TPU v7x, 128 devices: a whole 4x4x4 slice. The times are simulated.
128 devices in a mesh: row: 8 (over x, core), col: 16 (over z, y).
Axes of the slice: x: 4, y: 4, z: 4, core: 2. Of those that a mesh axis runs over, the one named last changes fastest.
Arguments:
- ham: bfloat16 [6144, 6144], P('row', 'col'), may hold values from -0.078125 to 0.078125
- deriv: bfloat16 [6144, 6144], P('row', 'col'), may hold values from -6 to 6
- band: int32 [48], replicated, may hold values from 1 to 24, as said below
- frag_of: int32 [48], replicated, may hold values from 0 to 31
Outputs:
- sign_iterate: bfloat16 [6144, 6144], P('row', 'col')
- energy_density: bfloat16 [6144, 6144], P('row', 'col')
- pulay_terms: float32 [32, 128], P('col')
Inputs may be any that keep to these rules, and one draw needn't show every extreme that they name: Some block row has band half-width exactly 24.
All inputs are finite; a program needn't handle non-finite values.
Results may differ from a plain program's by a relative error of at most 0.006.
Values may be sent and summed in bfloat16 or wider, within the bound.
A program may use at most 64 MiB of HBM per device.

v0:
```python
import jax
import jax.numpy as jnp
from jax import lax
from jax.sharding import PartitionSpec as P

BLK = 128
FRAG_DEV = 2


def column_panel_of(right_matrix):
    return lax.all_gather(right_matrix, "row", axis=0, tiled=True)


def folded_product(left_matrix, right_matrix):
    whole_panel = column_panel_of(right_matrix)
    return jnp.dot(
        lax.all_gather(left_matrix, "col", axis=1, tiled=True),
        whole_panel,
        preferred_element_type=jnp.float32,
    )


def body(ham, deriv, band, frag_of):
    rows_here = ham.shape[0]
    cols_here = ham.shape[1]
    block_rows = rows_here // BLK
    block_cols = cols_here // BLK
    row_index = lax.axis_index("row")
    col_index = lax.axis_index("col")
    row_blocks = row_index * block_rows + jnp.arange(block_rows, dtype=jnp.int32)
    col_blocks = col_index * block_cols + jnp.arange(block_cols, dtype=jnp.int32)
    row_band = lax.dynamic_slice_in_dim(band, row_index * block_rows, block_rows)
    col_band = lax.dynamic_slice_in_dim(band, col_index * block_cols, block_cols)
    widest = jnp.maximum(row_band[:, None], col_band[None, :])
    inside = jnp.abs(row_blocks[:, None] - col_blocks[None, :]) <= widest
    pattern = jnp.repeat(jnp.repeat(inside.astype(jnp.float32), BLK, axis=0), BLK, axis=1)
    global_rows = row_index * rows_here + jnp.arange(rows_here, dtype=jnp.int32)
    global_cols = col_index * cols_here + jnp.arange(cols_here, dtype=jnp.int32)
    identity = (global_rows[:, None] == global_cols[None, :]).astype(jnp.float32)
    start = (ham.astype(jnp.float32) * pattern).astype(jnp.bfloat16)

    def start_times(right_matrix):
        return folded_product(start, right_matrix)

    square = (start_times(start) * pattern).astype(jnp.bfloat16)
    cubic = start_times(square)
    sign_iterate = (pattern * (1.5 * start.astype(jnp.float32) - 0.5 * cubic)).astype(jnp.bfloat16)
    density = (0.5 * (identity - sign_iterate.astype(jnp.float32))).astype(jnp.bfloat16)
    weighted = (start_times(density) * pattern).astype(jnp.bfloat16)
    energy_density = (folded_product(density, weighted) * pattern).astype(jnp.bfloat16)
    column_terms = jnp.sum(energy_density.astype(jnp.float32) * deriv.astype(jnp.float32), axis=0)
    column_terms = column_terms.reshape(block_cols, BLK)
    local_frags = lax.dynamic_slice_in_dim(frag_of, col_index * block_cols, block_cols)
    fragment_count = FRAG_DEV * lax.axis_size("col")
    fragments = jnp.arange(fragment_count, dtype=jnp.int32)
    onehot = (local_frags[None, :] == fragments[:, None]).astype(jnp.float32)
    partial_value = jnp.dot(onehot, column_terms, precision=lax.Precision.HIGHEST)
    grand_total = lax.psum(partial_value, ("row", "col"))
    pulay_terms = lax.dynamic_slice_in_dim(grand_total, col_index * FRAG_DEV, FRAG_DEV, 0)
    return (sign_iterate, energy_density, pulay_terms)


def solution(mesh):
    placed = (P("row", "col"), P("row", "col"), P(), P())
    return jax.shard_map(
        body,
        mesh=mesh,
        in_specs=placed,
        out_specs=(P("row", "col"), P("row", "col"), P("col", None)),
        check_vma=False,
    )
```

profile of v0, /device:TPU:1, one launch (start us, length us, event | category | flops | bytes accessed | tf_op | source)
XLA Modules:
  0.0 432.5 jit_solution(7368020755092818838)
XLA Ops:
  7.2 0.0 all-gather.9.cloned.1.call-start
  7.2 0.7 dynamic_slice.13
  8.0 0.7 dynamic_slice.12
  8.7 0.1 fusion.9
  8.8 0.1 broadcast_bitcast_fusion
  8.9 0.1 broadcast_in_dim.5
  9.0 0.0 copy-start
  9.0 0.4 copy.8
  9.3 0.7 copy-done
  10.0 0.9 multiply_convert_fusion.1
  11.0 0.0 all-gather.9.cloned.1.call-update
  11.0 0.0 all-gather.7.cloned.1.call-start
  11.0 0.7 all-gather.7.cloned.1.call-update
  11.7 0.0 all-gather.11.cloned.1.call-start
  11.8 37.2 %all-gather.9.cloned.1.call-done = bf16[6144,384]{1,0:T(8,128)(2,1)} async-done(((bf16[768,384]{1,0:T(8,128)(2,1)}), bf16[6144,384]{1,0:T(8,128)(2,1)}) %all-gather.9.cloned.1.call-update) | async-done | bytes 4718608 | tf_op jit(solution)/shard_map/all_gather | solution.py:11
  48.9 83.6 %all-gather.7.cloned.1.call-done = bf16[768,6144]{1,0:T(8,128)(2,1)} async-done(((bf16[768,384]{1,0:T(8,128)(2,1)}), bf16[768,6144]{1,0:T(8,128)(2,1)}) %all-gather.7.cloned.1.call-update) | async-done | bytes 9437200 | tf_op jit(solution)/shard_map/all_gather | solution.py:17
  132.5 9.7 %fusion.3 = bf16[768,384]{0,1:T(8,128)(2,1)} fusion(f32[768,384]{0,1:T(8,128)S(1)} %bitcast.20, bf16[768,6144]{1,0:T(8,128)(2,1)} %all-gather.7.cloned.1.call-done, bf16[6144,384]{1,0:T(8,128)(2,1)} %all-gather.9.cloned.1.call-done), kind=kOutput, calls=%fused_computation.7 | convolution fusion | flops 3624468480 | bytes 15925248 | tf_op jit(solution)/shard_map/dot_general | solution.py:16
  142.2 0.0 all-gather.11.cloned.1.call-update
  142.3 0.0 all-gather.15.cloned.1.call-start
  142.3 35.3 %all-gather.11.cloned.1.call-done = bf16[6144,384]{0,1:T(8,128)(2,1)} async-done(((bf16[768,384]{0,1:T(8,128)(2,1)}), bf16[6144,384]{0,1:T(8,128)(2,1)}) %all-gather.11.cloned.1.call-update) | async-done | bytes 4718608 | tf_op jit(solution)/shard_map/all_gather | solution.py:11
  177.6 10.0 %multiply_convert_fusion = (bf16[768,384]{1,0:T(8,128)(2,1)}, bf16[768,384]{1,0:T(8,128)(2,1)}) fusion(s32[384]{0:T(512)S(1)} %iota_add_fusion.1, s32[768]{0:T(1024)S(1)} %iota_add_fusion, f32[768,384]{1,0:T(8,128)S(1)} %copy.8, bf16[768,6144]{1,0:T(8,128)(2,1)} %all-gather.7.cloned.1.call-done, bf16[6144,384]{0,1:T(8,128)(2,1)} %all-gather.11.cloned.1.call-done, ...), kind=kOutput, calls=%fused_computation.11 | convolution fusion | flops 3628302336 | bytes 17109504 | tf_op jit(solution)/shard_map/dot_general | solution.py:16
  187.6 0.0 all-gather.15.cloned.1.call-update
  187.6 0.0 all-gather.17.cloned.1.call-start
  187.7 34.3 %all-gather.15.cloned.1.call-done = bf16[6144,384]{1,0:T(8,128)(2,1)} async-done(((bf16[768,384]{1,0:T(8,128)(2,1)}), bf16[6144,384]{1,0:T(8,128)(2,1)}) %all-gather.15.cloned.1.call-update) | async-done | bytes 4718608 | tf_op jit(solution)/shard_map/all_gather | solution.py:11
  222.0 9.7 %fusion.4 = bf16[768,384]{0,1:T(8,128)(2,1)} fusion(f32[768,384]{0,1:T(8,128)S(1)} %bitcast.21, bf16[768,6144]{1,0:T(8,128)(2,1)} %all-gather.7.cloned.1.call-done, bf16[6144,384]{1,0:T(8,128)(2,1)} %all-gather.15.cloned.1.call-done), kind=kOutput, calls=%fused_computation.8 | convolution fusion | flops 3624468480 | bytes 15925248 | tf_op jit(solution)/shard_map/dot_general | solution.py:16
  231.7 0.0 copy-start.2
  231.7 0.0 copy-start.1
  231.7 0.0 all-gather.17.cloned.1.call-update
  231.7 0.2 all-gather.13.cloned.1.call-start
  231.9 0.3 all-gather.13.cloned.1.call-update
  232.3 0.0 copy-done.2
  232.3 0.1 dynamic_slice.14
  232.4 33.7 %all-gather.17.cloned.1.call-done = bf16[6144,384]{0,1:T(8,128)(2,1)} async-done(((bf16[768,384]{0,1:T(8,128)(2,1)}), bf16[6144,384]{0,1:T(8,128)(2,1)}) %all-gather.17.cloned.1.call-update) | async-done | bytes 4718608 | tf_op jit(solution)/shard_map/all_gather | solution.py:11
  266.1 83.4 %all-gather.13.cloned.1.call-done = bf16[768,6144]{1,0:T(8,128)(2,1)} async-done(((bf16[768,384]{1,0:T(8,128)(2,1)}), bf16[768,6144]{1,0:T(8,128)(2,1)}) %all-gather.13.cloned.1.call-update) | async-done | bytes 9437200 | tf_op jit(solution)/shard_map/all_gather | solution.py:17
  349.5 0.0 copy-done.1
  349.5 9.8 %multiply_reduce_fusion = (f32[384]{0:T(512)S(1)}, bf16[768,384]{1,0:T(8,128)(2,1)}) fusion(bf16[768,384]{1,0:T(8,128)(2,1)S(1)} %copy-done.1, f32[768,384]{1,0:T(8,128)S(1)} %copy.8, bf16[768,6144]{1,0:T(8,128)(2,1)} %all-gather.13.cloned.1.call-done, bf16[6144,384]{0,1:T(8,128)(2,1)} %all-gather.17.cloned.1.call-done), kind=kOutput, calls=%fused_computation.10 | convolution fusion | flops 3625647616 | bytes 16516608 | tf_op jit(solution)/shard_map/dot_general | solution.py:16
  359.3 0.1 fusion.6
  359.4 65.7 %psum.7 = f32[32,128]{1,0:T(8,128)S(1)} all-reduce(f32[32,128]{1,0:T(8,128)S(1)} %fusion.6), channel_id=1, replica_groups=mesh['row'=8,'col'=16] {'row','col'}, use_global_device_ids=true, to_apply=%region_1.0 | all-reduce | flops 4096 | bytes 32768 | tf_op jit(solution)/shard_map/psum | solution.py:58
  425.1 0.6 constant_dynamic-slice_fusion
  (5 shorter events, 0.0 us)
Async XLA Ops:
  7.2 41.8 %all-gather.9.cloned.1.call-start = ((), (), s32[]{:S(2)}) async-start(), calls=%async_computation.1 | async-start | bytes 5308416 | tf_op jit(solution)/shard_map/all_gather | solution.py:11
  9.0 1.1 copy-start
  11.0 121.6 %all-gather.7.cloned.1.call-start = ((), (), s32[]{:S(2)}) async-start(), calls=%async_computation | async-start | bytes 10027008 | tf_op jit(solution)/shard_map/all_gather | solution.py:17
  11.7 165.9 %all-gather.11.cloned.1.call-start = ((), (), s32[]{:S(2)}) async-start(), calls=%async_computation.2 | async-start | bytes 5308416 | tf_op jit(solution)/shard_map/all_gather | solution.py:11
  142.3 79.7 %all-gather.15.cloned.1.call-start = ((), (), s32[]{:S(2)}) async-start(), calls=%async_computation.4 | async-start | bytes 5308416 | tf_op jit(solution)/shard_map/all_gather | solution.py:11
  187.6 78.5 %all-gather.17.cloned.1.call-start = ((), (), s32[]{:S(2)}) async-start(), calls=%async_computation.5 | async-start | bytes 5308416 | tf_op jit(solution)/shard_map/all_gather | solution.py:11
  231.7 0.7 copy-start.2
  231.7 117.8 %copy-start.1 = (bf16[768,384]{1,0:T(8,128)(2,1)S(1)}, bf16[768,384]{1,0:T(8,128)(2,1)}, u32[]{:S(2)}) copy-start(bf16[768,384]{1,0:T(8,128)(2,1)} %param.5) | copy-start | bytes 1769476
  231.7 117.8 %all-gather.13.cloned.1.call-start = ((), (), s32[]{:S(2)}) async-start(), calls=%async_computation.3 | async-start | bytes 10027008 | tf_op jit(solution)/shard_map/all_gather | solution.py:17
Sparse Core Ops, SparseCore 0:
  11.1 37.7 all-gather.8
  51.6 80.8 all-gather.6
  142.4 35.1 all-gather.10
  187.7 34.2 all-gather.14
  231.8 34.2 all-gather.16
  268.6 80.8 all-gather.12
where the time goes:
time: 433 us
  waiting for transfers between devices  309 us (71%)
  blocking collectives  65.7 us (15%)
  matrix products  39.3 us (9%)
  between operations  14.2 us (3%)
    all_gather x2, waiting for transfers between devices, folded_product(): lax.all_gather(left_matrix, 'col', axis=1, tiled=True)  167 us
    all_gather x4, waiting for transfers between devices, column_panel_of(): return lax.all_gather(right_matrix, 'row', axis=0, tiled=True)  140 us
    psum x1, blocking collectives, body(): grand_total = lax.psum(partial_value, ('row', 'col'))  65.7 us
    dot_general x4, matrix products, folded_product(): jnp.dot(lax.all_gather(left_matrix, 'col', axis=1, tiled=True), whole_pan...  39.1 us
  transfers between devices with their start and end apart: 6, of which 6 were waited for; matrix products, arithmetic and copies ran while one was open for 0% of the time, Pallas kernels for 0%

commit v1 on v0

--- a/solution.py
+++ b/solution.py
@@ -13,10 +13,35 @@
 
 def folded_product(left_matrix, right_matrix):
     whole_panel = column_panel_of(right_matrix)
+
+    def record_show(sample, shard_axis):
+        g_now, x_next, item_now = (
+            lax.axis_size(shard_axis),
+            lax.axis_index(shard_axis),
+            sample.shape[1],
+        )
+        xs_all = list(map(lambda dev_i: (dev_i, (dev_i + 1) % g_now), range(g_now)))
+        windows = list(map(lambda dev_i: (dev_i, (dev_i - 1) % g_now), range(g_now)))
+        local_part = jnp.zeros(
+            (*sample.shape[:1], g_now * item_now, *sample.shape[2:]), sample.dtype
+        )
+        arr_out = block_next = sample
+        mixed_arr = g_now // 2
+        local_part = lax.dynamic_update_slice_in_dim(local_part, sample, x_next * item_now, axis=1)
+        for pp in [*range(1, mixed_arr + 1)]:
+            arr_out = lax.ppermute(arr_out, axis_name=shard_axis, perm=xs_all)
+            local_part = lax.dynamic_update_slice_in_dim(
+                local_part, arr_out, (x_next - pp) % g_now * item_now, axis=1
+            )
+            if pp < g_now - mixed_arr:
+                block_next = lax.ppermute(block_next, axis_name=shard_axis, perm=windows)
+                local_part = lax.dynamic_update_slice_in_dim(
+                    local_part, block_next, (x_next + pp) % g_now * item_now, axis=1
+                )
+        return local_part
+
     return jnp.dot(
-        lax.all_gather(left_matrix, "col", axis=1, tiled=True),
-        whole_panel,
-        preferred_element_type=jnp.float32,
+        record_show(left_matrix, shard_axis="col"), whole_panel, preferred_element_type=jnp.float32
     )
 
 

time: 433 us -> 453 us (1.046)
  waiting for transfers between devices: 309 us -> 202 us
  starting transfers between devices: 0.42 us -> 70.4 us
  local copies, waits for them, and re-layouts: 3.37 us -> 57.8 us
    all_gather x2 -> x0, waiting for transfers between devices: 167 us -> none  [folded_product(): lax.all_gather(left_matrix, 'col', axis=1, tiled=True)]
    ppermute x0 -> x30, waiting for transfers between devices: none -> 130 us  [the longest x16 130 us: record_show(): arr_out = lax.ppermute(arr_out, axis_name=shard_axis, perm=xs_all)]
    ppermute x0 -> x30, starting transfers between devices: none -> 70.2 us  [the longest x14 66.6 us: record_show(): block_next = lax.ppermute(block_next, axis_name=shard_axis, perm=windows)]
    all_gather x4, waiting for transfers between devices: 140 us -> 71.8 us  [column_panel_of(): return lax.all_gather(right_matrix, 'row', axis=0, tiled=True)]
    dynamic_update_slice x0 -> x30, local copies, waits for them, and re-layouts: none -> 45.4 us  [the longest x16 23.7 us: record_show(): lax.dynamic_update_slice_in_dim(local_part, arr_out, (x_next - pp) % g_no...]
    another operation x0 -> x2, local copies, waits for them, and re-layouts: none -> 9.64 us
  transfers between devices with their start and end apart: 6 -> 34, of which waited for: 6 -> 17; matrix products, arithmetic and copies ran while one was open for 0% -> 10% of each run, Pallas kernels for 0% -> 0%
where the time goes in v1:
time: 453 us; the launch traced here: 452 us
  waiting for transfers between devices  202 us (45%)
  starting transfers between devices  70.4 us (16%)
  blocking collectives  69.1 us (15%)
  local copies, waits for them, and re-layouts  57.8 us (13%)
  matrix products  38 us (8%)
  between operations  14 us (3%)
    ppermute x16, waiting for transfers between devices, record_show(): arr_out = lax.ppermute(arr_out, axis_name=shard_axis, perm=xs_all)  130 us
    all_gather x4, waiting for transfers between devices, column_panel_of(): return lax.all_gather(right_matrix, 'row', axis=0, tiled=True)  71.8 us
    psum x1, blocking collectives, body(): grand_total = lax.psum(partial_value, ('row', 'col'))  69.1 us
    ppermute x14, starting transfers between devices, record_show(): block_next = lax.ppermute(block_next, axis_name=shard_axis, perm=windows)  66.6 us
    dot_general x4, matrix products, folded_product(): jnp.dot(record_show(left_matrix, shard_axis='col'), whole_panel, preferre...  37.9 us
    dynamic_update_slice x16, local copies, waits for them, and re-layouts, record_show(): lax.dynamic_update_slice_in_dim(local_part, arr_out, (x_next - pp) % g_no...  23.7 us
    dynamic_update_slice x14, local copies, waits for them, and re-layouts, record_show(): lax.dynamic_update_slice_in_dim(local_part, block_next, (x_next + pp) % g...  21.7 us
    another operation x2, local copies, waits for them, and re-layouts  9.64 us
  transfers between devices with their start and end apart: 34, of which 17 were waited for; matrix products, arithmetic and copies ran while one was open for 10% of the time, Pallas kernels for 0%

profile of v1, /device:TPU:1, one launch (start us, length us, event | category | flops | bytes accessed | tf_op | source)
XLA Modules:
  0.0 452.1 jit_solution(13396589840212585847)
XLA Ops:
  9.4 4.8 %broadcast.40.clone = bf16[768,6144]{1,0:T(8,128)(2,1)} broadcast(bf16[]{:T(256)} %constant.196.clone.1), dimensions={} | broadcast | bytes 9437186 | tf_op jit(solution)/shard_map/broadcast.3
  15.5 2.3 collective-permute-start
  17.8 4.9 %collective-permute-start.1 = (bf16[768,384]{1,0:T(8,128)(2,1)}, bf16[768,384]{1,0:T(8,128)(2,1)S(1)}, u32[]{:S(2)}, u32[]{:S(2)}) collective-permute-start(bf16[768,384]{1,0:T(8,128)(2,1)} %get-tuple-element.6), channel_id=1, source_target_pairs={{0,15},{1,0},{2,1},{3,2},{4,3},{5,4},{6,5},{7,6},{8,7},{9,8},{10,9... | collective-permute-start | bytes 1769480 | tf_op jit(solution)/shard_map/ppermute | solution.py:37
  22.7 13.2 %collective-permute-done = bf16[768,384]{1,0:T(8,128)(2,1)S(1)} collective-permute-done((bf16[768,384]{1,0:T(8,128)(2,1)}, bf16[768,384]{1,0:T(8,128)(2,1)S(1)}, u32[]{:S(2)}, u32[]{:S(2)}) %collective-permute-start) | collective-permute-done | bytes 589856 | tf_op jit(solution)/shard_map/ppermute | solution.py:32
  35.9 4.8 %collective-permute-start.3 = (bf16[768,384]{1,0:T(8,128)(2,1)S(1)}, bf16[768,384]{1,0:T(8,128)(2,1)S(1)}, u32[]{:S(2)}, u32[]{:S(2)}) collective-permute-start(bf16[768,384]{1,0:T(8,128)(2,1)S(1)} %collective-permute-done.1), channel_id=1, source_target_pairs={{0,15},{1,0},{2,1},{3,2},{4,3},{5,4},{6,5},{7,6},{8,7},{9,8},{10,9... | collective-permute-start | bytes 1769480 | tf_op jit(solution)/shard_map/ppermute | solution.py:37
  40.6 12.2 %collective-permute-done.2 = bf16[768,384]{1,0:T(8,128)(2,1)S(1)} collective-permute-done((bf16[768,384]{1,0:T(8,128)(2,1)S(1)}, bf16[768,384]{1,0:T(8,128)(2,1)S(1)}, u32[]{:S(2)}, u32[]{:S(2)}) %collective-permute-start.2) | collective-permute-done | bytes 589856 | tf_op jit(solution)/shard_map/ppermute | solution.py:32
  52.8 4.8 %collective-permute-start.5 = (bf16[768,384]{1,0:T(8,128)(2,1)S(1)}, bf16[768,384]{1,0:T(8,128)(2,1)S(1)}, u32[]{:S(2)}, u32[]{:S(2)}) collective-permute-start(bf16[768,384]{1,0:T(8,128)(2,1)S(1)} %collective-permute-done.3), channel_id=1, source_target_pairs={{0,15},{1,0},{2,1},{3,2},{4,3},{5,4},{6,5},{7,6},{8,7},{9,8},{10,9... | collective-permute-start | bytes 1769480 | tf_op jit(solution)/shard_map/ppermute | solution.py:37
  57.6 11.3 %collective-permute-done.4 = bf16[768,384]{1,0:T(8,128)(2,1)S(1)} collective-permute-done((bf16[768,384]{1,0:T(8,128)(2,1)S(1)}, bf16[768,384]{1,0:T(8,128)(2,1)S(1)}, u32[]{:S(2)}, u32[]{:S(2)}) %collective-permute-start.4) | collective-permute-done | bytes 589856 | tf_op jit(solution)/shard_map/ppermute | solution.py:32
  68.9 4.8 %collective-permute-start.7 = (bf16[768,384]{1,0:T(8,128)(2,1)S(1)}, bf16[768,384]{1,0:T(8,128)(2,1)}, u32[]{:S(2)}, u32[]{:S(2)}) collective-permute-start(bf16[768,384]{1,0:T(8,128)(2,1)S(1)} %collective-permute-done.5), channel_id=1, source_target_pairs={{0,15},{1,0},{2,1},{3,2},{4,3},{5,4},{6,5},{7,6},{8,7},{9,8},{10,9... | collective-permute-start | bytes 1769480 | tf_op jit(solution)/shard_map/ppermute | solution.py:37
  73.7 10.5 %collective-permute-done.6 = bf16[768,384]{1,0:T(8,128)(2,1)S(1)} collective-permute-done((bf16[768,384]{1,0:T(8,128)(2,1)S(1)}, bf16[768,384]{1,0:T(8,128)(2,1)S(1)}, u32[]{:S(2)}, u32[]{:S(2)}) %collective-permute-start.6) | collective-permute-done | bytes 589856 | tf_op jit(solution)/shard_map/ppermute | solution.py:32
  84.2 4.8 %collective-permute-start.9 = (bf16[768,384]{1,0:T(8,128)(2,1)}, bf16[768,384]{1,0:T(8,128)(2,1)}, u32[]{:S(2)}, u32[]{:S(2)}) collective-permute-start(bf16[768,384]{1,0:T(8,128)(2,1)} %collective-permute-done.7), channel_id=1, source_target_pairs={{0,15},{1,0},{2,1},{3,2},{4,3},{5,4},{6,5},{7,6},{8,7},{9,8},{10,9... | collective-permute-start | bytes 1769480 | tf_op jit(solution)/shard_map/ppermute | solution.py:37
  89.0 9.6 %collective-permute-done.8 = bf16[768,384]{1,0:T(8,128)(2,1)} collective-permute-done((bf16[768,384]{1,0:T(8,128)(2,1)S(1)}, bf16[768,384]{1,0:T(8,128)(2,1)}, u32[]{:S(2)}, u32[]{:S(2)}) %collective-permute-start.8) | collective-permute-done | bytes 589856 | tf_op jit(solution)/shard_map/ppermute | solution.py:32
  99.6 2.1 constant_dynamic-update-slice_fusion.29
  103.7 4.7 %collective-permute-start.11 = (bf16[768,384]{1,0:T(8,128)(2,1)}, bf16[768,384]{1,0:T(8,128)(2,1)S(1)}, u32[]{:S(2)}, u32[]{:S(2)}) collective-permute-start(bf16[768,384]{1,0:T(8,128)(2,1)} %collective-permute-done.9), channel_id=1, source_target_pairs={{0,15},{1,0},{2,1},{3,2},{4,3},{5,4},{6,5},{7,6},{8,7},{9,8},{10,9... | collective-permute-start | bytes 1769480 | tf_op jit(solution)/shard_map/ppermute | solution.py:37
  108.4 2.0 constant_dynamic-update-slice_fusion.27
  110.4 2.1 collective-permute-done.10
  117.4 2.0 constant_dynamic-update-slice_fusion.23
  119.4 4.7 %collective-permute-start.13 = (bf16[768,384]{1,0:T(8,128)(2,1)S(1)}, bf16[768,384]{1,0:T(8,128)(2,1)S(1)}, u32[]{:S(2)}, u32[]{:S(2)}) collective-permute-start(bf16[768,384]{1,0:T(8,128)(2,1)S(1)} %collective-permute-done.11), channel_id=1, source_target_pairs={{0,15},{1,0},{2,1},{3,2},{4,3},{5,4},{6,5},{7,6},{8,7},{9,8},{10,9... | collective-permute-start | bytes 1769480 | tf_op jit(solution)/shard_map/ppermute | solution.py:37
  126.2 2.0 constant_dynamic-update-slice_fusion.21
  128.2 2.1 constant_dynamic-update-slice_fusion.20
  133.1 5.2 %collective-permute-done.14 = bf16[768,384]{1,0:T(8,128)(2,1)S(1)} collective-permute-done((bf16[768,384]{1,0:T(8,128)(2,1)S(1)}, bf16[768,384]{1,0:T(8,128)(2,1)S(1)}, u32[]{:S(2)}, u32[]{:S(2)}) %collective-permute-start.14) | collective-permute-done | bytes 589856 | tf_op jit(solution)/shard_map/ppermute | solution.py:32
  139.2 9.7 %fusion.3 = bf16[768,384]{0,1:T(8,128)(2,1)} fusion(f32[768,384]{0,1:T(8,128)S(1)} %bitcast.20, bf16[768,6144]{1,0:T(8,128)(2,1)} %constant_dynamic-update-slice_fusion.16, bf16[6144,384]{1,0:T(8,128)(2,1)} %all-gather.5.cloned.1.call-done), kind=kOutput, calls=%fused_computation.7 | convolution fusion | flops 3624468480 | bytes 15925248 | tf_op jit(solution)/shard_map/dot_general | solution.py:43
  149.0 37.5 %all-gather.7.cloned.1.call-done = bf16[6144,384]{0,1:T(8,128)(2,1)} async-done(((bf16[768,384]{0,1:T(8,128)(2,1)}), bf16[6144,384]{0,1:T(8,128)(2,1)}) %all-gather.7.cloned.1.call-update) | async-done | bytes 4718608 | tf_op jit(solution)/shard_map/all_gather | solution.py:11
  186.5 4.8 %broadcast.40 = bf16[768,6144]{1,0:T(8,128)(2,1)} broadcast(bf16[]{:T(256)} %constant.196.clone.1), dimensions={} | broadcast | bytes 9437186 | tf_op jit(solution)/shard_map/broadcast.3
  191.3 8.6 %constant_dynamic-update-slice_fusion.15 = (bf16[768,6144]{1,0:T(8,128)(2,1)}, bf16[768,384]{1,0:T(8,128)(2,1)}, bf16[768,384]{1,0:T(8,128)(2,1)}) fusion(bf16[768,6144]{1,0:T(8,128)(2,1)} %broadcast.40, s32[]{:T(128)S(6)} %select_n.261, s32[384]{0:T(512)S(1)} %iota_add_fusion.1, s32[768]{0:T(1024)S(1)} %iota_add_fusion, f32[768,384]{1,0:T(8,128)S(1)} %copy.8, ...), kind=kOutput, calls=%fused_computation.32 | convolution fusion | flops 3627417600 | bytes 17699332 | tf_op jit(solution)/shard_map/dot_general | solution.py:43
  200.1 34.3 %all-gather.9.cloned.1.call-done = bf16[6144,384]{1,0:T(8,128)(2,1)} async-done(((bf16[768,384]{1,0:T(8,128)(2,1)}), bf16[6144,384]{1,0:T(8,128)(2,1)}) %all-gather.9.cloned.1.call-update) | async-done | bytes 4718608 | tf_op jit(solution)/shard_map/all_gather | solution.py:11
  234.4 9.7 %fusion.4 = bf16[768,384]{0,1:T(8,128)(2,1)} fusion(f32[768,384]{0,1:T(8,128)S(1)} %bitcast.21, bf16[768,6144]{1,0:T(8,128)(2,1)} %constant_dynamic-update-slice_fusion.16, bf16[6144,384]{1,0:T(8,128)(2,1)} %all-gather.9.cloned.1.call-done), kind=kOutput, calls=%fused_computation.8 | convolution fusion | flops 3624468480 | bytes 15925248 | tf_op jit(solution)/shard_map/dot_general | solution.py:43
  245.4 3.9 collective-permute-start.16
  249.3 12.9 %collective-permute-done.15 = bf16[768,384]{1,0:T(8,128)(2,1)S(1)} collective-permute-done((bf16[768,384]{1,0:T(8,128)(2,1)S(1)}, bf16[768,384]{1,0:T(8,128)(2,1)S(1)}, u32[]{:S(2)}, u32[]{:S(2)}) %collective-permute-start.15) | collective-permute-done | bytes 589856 | tf_op jit(solution)/shard_map/ppermute | solution.py:32
  262.2 5.0 %collective-permute-start.18 = (bf16[768,384]{1,0:T(8,128)(2,1)S(1)}, bf16[768,384]{1,0:T(8,128)(2,1)S(1)}, u32[]{:S(2)}, u32[]{:S(2)}) collective-permute-start(bf16[768,384]{1,0:T(8,128)(2,1)S(1)} %collective-permute-done.16), channel_id=1, source_target_pairs={{0,15},{1,0},{2,1},{3,2},{4,3},{5,4},{6,5},{7,6},{8,7},{9,8},{10,9... | collective-permute-start | bytes 1769480 | tf_op jit(solution)/shard_map/ppermute | solution.py:37
  267.2 12.1 %collective-permute-done.17 = bf16[768,384]{1,0:T(8,128)(2,1)S(1)} collective-permute-done((bf16[768,384]{1,0:T(8,128)(2,1)S(1)}, bf16[768,384]{1,0:T(8,128)(2,1)S(1)}, u32[]{:S(2)}, u32[]{:S(2)}) %collective-permute-start.17) | collective-permute-done | bytes 589856 | tf_op jit(solution)/shard_map/ppermute | solution.py:32
  279.4 4.9 %collective-permute-start.20 = (bf16[768,384]{1,0:T(8,128)(2,1)S(1)}, bf16[768,384]{1,0:T(8,128)(2,1)S(1)}, u32[]{:S(2)}, u32[]{:S(2)}) collective-permute-start(bf16[768,384]{1,0:T(8,128)(2,1)S(1)} %collective-permute-done.18), channel_id=1, source_target_pairs={{0,15},{1,0},{2,1},{3,2},{4,3},{5,4},{6,5},{7,6},{8,7},{9,8},{10,9... | collective-permute-start | bytes 1769480 | tf_op jit(solution)/shard_map/ppermute | solution.py:37
  284.3 11.3 %collective-permute-done.19 = bf16[768,384]{1,0:T(8,128)(2,1)S(1)} collective-permute-done((bf16[768,384]{1,0:T(8,128)(2,1)S(1)}, bf16[768,384]{1,0:T(8,128)(2,1)S(1)}, u32[]{:S(2)}, u32[]{:S(2)}) %collective-permute-start.19) | collective-permute-done | bytes 589856 | tf_op jit(solution)/shard_map/ppermute | solution.py:32
  295.7 4.8 %collective-permute-start.22 = (bf16[768,384]{1,0:T(8,128)(2,1)S(1)}, bf16[768,384]{1,0:T(8,128)(2,1)}, u32[]{:S(2)}, u32[]{:S(2)}) collective-permute-start(bf16[768,384]{1,0:T(8,128)(2,1)S(1)} %collective-permute-done.20), channel_id=1, source_target_pairs={{0,15},{1,0},{2,1},{3,2},{4,3},{5,4},{6,5},{7,6},{8,7},{9,8},{10,9... | collective-permute-start | bytes 1769480 | tf_op jit(solution)/shard_map/ppermute | solution.py:37
  300.5 10.6 %collective-permute-done.21 = bf16[768,384]{1,0:T(8,128)(2,1)S(1)} collective-permute-done((bf16[768,384]{1,0:T(8,128)(2,1)S(1)}, bf16[768,384]{1,0:T(8,128)(2,1)S(1)}, u32[]{:S(2)}, u32[]{:S(2)}) %collective-permute-start.21) | collective-permute-done | bytes 589856 | tf_op jit(solution)/shard_map/ppermute | solution.py:32
  311.1 4.8 %collective-permute-start.24 = (bf16[768,384]{1,0:T(8,128)(2,1)}, bf16[768,384]{1,0:T(8,128)(2,1)S(1)}, u32[]{:S(2)}, u32[]{:S(2)}) collective-permute-start(bf16[768,384]{1,0:T(8,128)(2,1)} %collective-permute-done.22), channel_id=1, source_target_pairs={{0,15},{1,0},{2,1},{3,2},{4,3},{5,4},{6,5},{7,6},{8,7},{9,8},{10,9... | collective-permute-start | bytes 1769480 | tf_op jit(solution)/shard_map/ppermute | solution.py:37
  315.9 9.8 %collective-permute-done.23 = bf16[768,384]{1,0:T(8,128)(2,1)} collective-permute-done((bf16[768,384]{1,0:T(8,128)(2,1)S(1)}, bf16[768,384]{1,0:T(8,128)(2,1)}, u32[]{:S(2)}, u32[]{:S(2)}) %collective-permute-start.23) | collective-permute-done | bytes 589856 | tf_op jit(solution)/shard_map/ppermute | solution.py:32
  328.8 2.0 constant_dynamic-update-slice_fusion.12
  330.9 4.8 %collective-permute-start.26 = (bf16[768,384]{1,0:T(8,128)(2,1)S(1)}, bf16[768,384]{1,0:T(8,128)(2,1)S(1)}, u32[]{:S(2)}, u32[]{:S(2)}) collective-permute-start(bf16[768,384]{1,0:T(8,128)(2,1)S(1)} %collective-permute-done.24), channel_id=1, source_target_pairs={{0,15},{1,0},{2,1},{3,2},{4,3},{5,4},{6,5},{7,6},{8,7},{9,8},{10,9... | collective-permute-start | bytes 1769480 | tf_op jit(solution)/shard_map/ppermute | solution.py:37
  337.6 2.2 collective-permute-done.25
  341.7 2.0 constant_dynamic-update-slice_fusion.8
  343.7 2.0 constant_dynamic-update-slice_fusion.7
  345.7 4.7 %collective-permute-start.28 = (bf16[768,384]{1,0:T(8,128)(2,1)S(1)}, bf16[768,384]{1,0:T(8,128)(2,1)S(1)}, u32[]{:S(2)}, u32[]{:S(2)}) collective-permute-start(bf16[768,384]{1,0:T(8,128)(2,1)S(1)} %collective-permute-done.26), channel_id=1, source_target_pairs={{0,15},{1,0},{2,1},{3,2},{4,3},{5,4},{6,5},{7,6},{8,7},{9,8},{10,9... | collective-permute-start | bytes 1769480 | tf_op jit(solution)/shard_map/ppermute | solution.py:37
  350.5 2.0 constant_dynamic-update-slice_fusion.6
  353.8 2.0 constant_dynamic-update-slice_fusion.4
  358.6 6.3 %collective-permute-done.29 = bf16[768,384]{1,0:T(8,128)(2,1)S(1)} collective-permute-done((bf16[768,384]{1,0:T(8,128)(2,1)S(1)}, bf16[768,384]{1,0:T(8,128)(2,1)S(1)}, u32[]{:S(2)}, u32[]{:S(2)}) %collective-permute-start.29) | collective-permute-done | bytes 589856 | tf_op jit(solution)/shard_map/ppermute | solution.py:32
  365.9 9.9 %multiply_reduce_fusion = (f32[384]{0:T(512)S(1)}, bf16[768,384]{1,0:T(8,128)(2,1)}) fusion(bf16[768,384]{1,0:T(8,128)(2,1)} %param.5, f32[768,384]{1,0:T(8,128)S(1)} %copy.8, bf16[768,6144]{1,0:T(8,128)(2,1)} %constant_dynamic-update-slice_fusion, bf16[6144,384]{0,1:T(8,128)(2,1)} %all-gather.11.cloned.1.call-done), kind=kOutput, calls=%fused_computation.10 | convolution fusion | flops 3625647616 | bytes 16516608 | tf_op jit(solution)/shard_map/dot_general | solution.py:43
  375.9 69.1 %psum.7 = f32[32,128]{1,0:T(8,128)S(1)} all-reduce(f32[32,128]{1,0:T(8,128)S(1)} %fusion.6), channel_id=1, replica_groups=mesh['row'=8,'col'=16] {'row','col'}, use_global_device_ids=true, to_apply=%region_1.2 | all-reduce | flops 4096 | bytes 32768 | tf_op jit(solution)/shard_map/psum | solution.py:83
  (104 shorter events, 31.2 us)
Async XLA Ops:
  7.2 7.1 %copy-start.11 = (bf16[768,384]{1,0:T(8,128)(2,1)S(1)}, bf16[768,384]{1,0:T(8,128)(2,1)}, u32[]{:S(2)}) copy-start(bf16[768,384]{1,0:T(8,128)(2,1)} %param.4) | copy-start | bytes 1769476
  7.2 132.0 %all-gather.5.cloned.1.call-start = ((), (), s32[]{:S(2)}) async-start(), calls=%async_computation | async-start | bytes 5308416 | tf_op jit(solution)/shard_map/all_gather | solution.py:11
  15.5 171.0 %all-gather.7.cloned.1.call-start = ((), (), s32[]{:S(2)}) async-start(), calls=%async_computation.1 | async-start | bytes 5308416 | tf_op jit(solution)/shard_map/all_gather | solution.py:11
  15.5 20.3 %collective-permute-start = (bf16[768,384]{1,0:T(8,128)(2,1)}, bf16[768,384]{1,0:T(8,128)(2,1)S(1)}, u32[]{:S(2)}, u32[]{:S(2)}) collective-permute-start(bf16[768,384]{1,0:T(8,128)(2,1)} %get-tuple-element.6), channel_id=1, source_target_pairs={{0,1},{1,2},{2,3},{3,4},{4,5},{5,6},{6,7},{7,8},{8,9},{9,10},{10,1... | collective-permute-start | bytes 1769480 | tf_op jit(solution)/shard_map/ppermute | solution.py:32
  17.8 18.1 %collective-permute-start.1 = (bf16[768,384]{1,0:T(8,128)(2,1)}, bf16[768,384]{1,0:T(8,128)(2,1)S(1)}, u32[]{:S(2)}, u32[]{:S(2)}) collective-permute-start(bf16[768,384]{1,0:T(8,128)(2,1)} %get-tuple-element.6), channel_id=1, source_target_pairs={{0,15},{1,0},{2,1},{3,2},{4,3},{5,4},{6,5},{7,6},{8,7},{9,8},{10,9... | collective-permute-start | bytes 1769480 | tf_op jit(solution)/shard_map/ppermute | solution.py:37
  35.8 17.0 %collective-permute-start.2 = (bf16[768,384]{1,0:T(8,128)(2,1)S(1)}, bf16[768,384]{1,0:T(8,128)(2,1)S(1)}, u32[]{:S(2)}, u32[]{:S(2)}) collective-permute-start(bf16[768,384]{1,0:T(8,128)(2,1)S(1)} %collective-permute-done), channel_id=1, source_target_pairs={{0,1},{1,2},{2,3},{3,4},{4,5},{5,6},{6,7},{7,8},{8,9},{9,10},{10,1... | collective-permute-start | bytes 1769480 | tf_op jit(solution)/shard_map/ppermute | solution.py:32
  35.8 48.3 %copy-start.1 = (bf16[768,384]{1,0:T(8,128)(2,1)}, bf16[768,384]{1,0:T(8,128)(2,1)S(1)}, u32[]{:S(2)}) copy-start(bf16[768,384]{1,0:T(8,128)(2,1)S(1)} %collective-permute-done.1) | copy-start | bytes 1769476
  35.9 17.0 %collective-permute-start.3 = (bf16[768,384]{1,0:T(8,128)(2,1)S(1)}, bf16[768,384]{1,0:T(8,128)(2,1)S(1)}, u32[]{:S(2)}, u32[]{:S(2)}) collective-permute-start(bf16[768,384]{1,0:T(8,128)(2,1)S(1)} %collective-permute-done.1), channel_id=1, source_target_pairs={{0,15},{1,0},{2,1},{3,2},{4,3},{5,4},{6,5},{7,6},{8,7},{9,8},{10,9... | collective-permute-start | bytes 1769480 | tf_op jit(solution)/shard_map/ppermute | solution.py:37
  52.8 36.2 %copy-start.4 = (bf16[768,384]{1,0:T(8,128)(2,1)}, bf16[768,384]{1,0:T(8,128)(2,1)S(1)}, u32[]{:S(2)}) copy-start(bf16[768,384]{1,0:T(8,128)(2,1)S(1)} %collective-permute-done.2) | copy-start | bytes 1769476
  52.8 16.1 %collective-permute-start.4 = (bf16[768,384]{1,0:T(8,128)(2,1)S(1)}, bf16[768,384]{1,0:T(8,128)(2,1)S(1)}, u32[]{:S(2)}, u32[]{:S(2)}) collective-permute-start(bf16[768,384]{1,0:T(8,128)(2,1)S(1)} %collective-permute-done.2), channel_id=1, source_target_pairs={{0,1},{1,2},{2,3},{3,4},{4,5},{5,6},{6,7},{7,8},{8,9},{9,10},{10,1... | collective-permute-start | bytes 1769480 | tf_op jit(solution)/shard_map/ppermute | solution.py:32
  52.8 31.4 %copy-start.2 = (bf16[768,384]{1,0:T(8,128)(2,1)}, bf16[768,384]{1,0:T(8,128)(2,1)S(1)}, u32[]{:S(2)}) copy-start(bf16[768,384]{1,0:T(8,128)(2,1)S(1)} %collective-permute-done.3) | copy-start | bytes 1769476
  52.8 16.1 %collective-permute-start.5 = (bf16[768,384]{1,0:T(8,128)(2,1)S(1)}, bf16[768,384]{1,0:T(8,128)(2,1)S(1)}, u32[]{:S(2)}, u32[]{:S(2)}) collective-permute-start(bf16[768,384]{1,0:T(8,128)(2,1)S(1)} %collective-permute-done.3), channel_id=1, source_target_pairs={{0,15},{1,0},{2,1},{3,2},{4,3},{5,4},{6,5},{7,6},{8,7},{9,8},{10,9... | collective-permute-start | bytes 1769480 | tf_op jit(solution)/shard_map/ppermute | solution.py:37
  68.9 15.2 %collective-permute-start.6 = (bf16[768,384]{1,0:T(8,128)(2,1)S(1)}, bf16[768,384]{1,0:T(8,128)(2,1)S(1)}, u32[]{:S(2)}, u32[]{:S(2)}) collective-permute-start(bf16[768,384]{1,0:T(8,128)(2,1)S(1)} %collective-permute-done.4), channel_id=1, source_target_pairs={{0,1},{1,2},{2,3},{3,4},{4,5},{5,6},{6,7},{7,8},{8,9},{9,10},{10,1... | collective-permute-start | bytes 1769480 | tf_op jit(solution)/shard_map/ppermute | solution.py:32
  68.9 15.3 %copy-start.3 = (bf16[768,384]{1,0:T(8,128)(2,1)}, bf16[768,384]{1,0:T(8,128)(2,1)S(1)}, u32[]{:S(2)}) copy-start(bf16[768,384]{1,0:T(8,128)(2,1)S(1)} %collective-permute-done.5) | copy-start | bytes 1769476
  68.9 15.3 %collective-permute-start.7 = (bf16[768,384]{1,0:T(8,128)(2,1)S(1)}, bf16[768,384]{1,0:T(8,128)(2,1)}, u32[]{:S(2)}, u32[]{:S(2)}) collective-permute-start(bf16[768,384]{1,0:T(8,128)(2,1)S(1)} %collective-permute-done.5), channel_id=1, source_target_pairs={{0,15},{1,0},{2,1},{3,2},{4,3},{5,4},{6,5},{7,6},{8,7},{9,8},{10,9... | collective-permute-start | bytes 1769480 | tf_op jit(solution)/shard_map/ppermute | solution.py:37
  84.2 14.5 %copy-start.5 = (bf16[768,384]{1,0:T(8,128)(2,1)}, bf16[768,384]{1,0:T(8,128)(2,1)S(1)}, u32[]{:S(2)}) copy-start(bf16[768,384]{1,0:T(8,128)(2,1)S(1)} %collective-permute-done.6) | copy-start | bytes 1769476
  84.2 14.5 %collective-permute-start.8 = (bf16[768,384]{1,0:T(8,128)(2,1)S(1)}, bf16[768,384]{1,0:T(8,128)(2,1)}, u32[]{:S(2)}, u32[]{:S(2)}) collective-permute-start(bf16[768,384]{1,0:T(8,128)(2,1)S(1)} %collective-permute-done.6), channel_id=1, source_target_pairs={{0,1},{1,2},{2,3},{3,4},{4,5},{5,6},{6,7},{7,8},{8,9},{9,10},{10,1... | collective-permute-start | bytes 1769480 | tf_op jit(solution)/shard_map/ppermute | solution.py:32
  84.2 19.5 %collective-permute-start.9 = (bf16[768,384]{1,0:T(8,128)(2,1)}, bf16[768,384]{1,0:T(8,128)(2,1)}, u32[]{:S(2)}, u32[]{:S(2)}) collective-permute-start(bf16[768,384]{1,0:T(8,128)(2,1)} %collective-permute-done.7), channel_id=1, source_target_pairs={{0,15},{1,0},{2,1},{3,2},{4,3},{5,4},{6,5},{7,6},{8,7},{9,8},{10,9... | collective-permute-start | bytes 1769480 | tf_op jit(solution)/shard_map/ppermute | solution.py:37
  98.7 13.8 %collective-permute-start.10 = (bf16[768,384]{1,0:T(8,128)(2,1)}, bf16[768,384]{1,0:T(8,128)(2,1)}, u32[]{:S(2)}, u32[]{:S(2)}) collective-permute-start(bf16[768,384]{1,0:T(8,128)(2,1)} %collective-permute-done.8), channel_id=1, source_target_pairs={{0,1},{1,2},{2,3},{3,4},{4,5},{5,6},{6,7},{7,8},{8,9},{9,10},{10,1... | collective-permute-start | bytes 1769480 | tf_op jit(solution)/shard_map/ppermute | solution.py:32
  103.7 15.8 %collective-permute-start.11 = (bf16[768,384]{1,0:T(8,128)(2,1)}, bf16[768,384]{1,0:T(8,128)(2,1)S(1)}, u32[]{:S(2)}, u32[]{:S(2)}) collective-permute-start(bf16[768,384]{1,0:T(8,128)(2,1)} %collective-permute-done.9), channel_id=1, source_target_pairs={{0,15},{1,0},{2,1},{3,2},{4,3},{5,4},{6,5},{7,6},{8,7},{9,8},{10,9... | collective-permute-start | bytes 1769480 | tf_op jit(solution)/shard_map/ppermute | solution.py:37
  112.5 13.7 %collective-permute-start.12 = (bf16[768,384]{1,0:T(8,128)(2,1)}, bf16[768,384]{1,0:T(8,128)(2,1)S(1)}, u32[]{:S(2)}, u32[]{:S(2)}) collective-permute-start(bf16[768,384]{1,0:T(8,128)(2,1)} %collective-permute-done.10), channel_id=1, source_target_pairs={{0,1},{1,2},{2,3},{3,4},{4,5},{5,6},{6,7},{7,8},{8,9},{9,10},{10,1... | collective-permute-start | bytes 1769480 | tf_op jit(solution)/shard_map/ppermute | solution.py:32
  119.4 12.7 %collective-permute-start.13 = (bf16[768,384]{1,0:T(8,128)(2,1)S(1)}, bf16[768,384]{1,0:T(8,128)(2,1)S(1)}, u32[]{:S(2)}, u32[]{:S(2)}) collective-permute-start(bf16[768,384]{1,0:T(8,128)(2,1)S(1)} %collective-permute-done.11), channel_id=1, source_target_pairs={{0,15},{1,0},{2,1},{3,2},{4,3},{5,4},{6,5},{7,6},{8,7},{9,8},{10,9... | collective-permute-start | bytes 1769480 | tf_op jit(solution)/shard_map/ppermute | solution.py:37
  126.2 12.1 %collective-permute-start.14 = (bf16[768,384]{1,0:T(8,128)(2,1)S(1)}, bf16[768,384]{1,0:T(8,128)(2,1)S(1)}, u32[]{:S(2)}, u32[]{:S(2)}) collective-permute-start(bf16[768,384]{1,0:T(8,128)(2,1)S(1)} %collective-permute-done.12), channel_id=1, source_target_pairs={{0,1},{1,2},{2,3},{3,4},{4,5},{5,6},{6,7},{7,8},{8,9},{9,10},{10,1... | collective-permute-start | bytes 1769480 | tf_op jit(solution)/shard_map/ppermute | solution.py:32
  148.9 42.5 %copy-start = (bf16[768,384]{1,0:T(8,128)(2,1)S(1)}, bf16[768,384]{1,0:T(8,128)(2,1)}, u32[]{:S(2)}) copy-start(bf16[768,384]{1,0:T(8,128)(2,1)} %get-tuple-element.6) | copy-start | bytes 1769476
  148.9 85.5 %all-gather.9.cloned.1.call-start = ((), (), s32[]{:S(2)}) async-start(), calls=%async_computation.2 | async-start | bytes 5308416 | tf_op jit(solution)/shard_map/all_gather | solution.py:11
  186.5 4.8 %copy-start.12 = (bf16[6144,384]{0,1:T(8,128)(2,1)S(1)}, bf16[6144,384]{0,1:T(8,128)(2,1)}, u32[]{:S(2)}) copy-start(bf16[6144,384]{0,1:T(8,128)(2,1)} %all-gather.7.cloned.1.call-done) | copy-start | bytes 14155780
  200.0 44.1 %copy-start.10 = (bf16[768,384]{1,0:T(8,128)(2,1)S(1)}, bf16[768,384]{1,0:T(8,128)(2,1)}, u32[]{:S(2)}) copy-start(bf16[768,384]{1,0:T(8,128)(2,1)} %get-tuple-element.4) | copy-start | bytes 1769476
  200.0 125.7 %copy-start.13 = (s32[48]{0:T(128)S(1)}, s32[48]{0:T(128)}, u32[]{:S(2)}) copy-start(s32[48]{0:T(128)} %param.7) | copy-start | bytes 580
  200.0 165.9 %all-gather.11.cloned.1.call-start = ((), (), s32[]{:S(2)}) async-start(), calls=%async_computation.3 | async-start | bytes 5308416 | tf_op jit(solution)/shard_map/all_gather | solution.py:11
  244.1 18.1 %collective-permute-start.15 = (bf16[768,384]{1,0:T(8,128)(2,1)S(1)}, bf16[768,384]{1,0:T(8,128)(2,1)S(1)}, u32[]{:S(2)}, u32[]{:S(2)}) collective-permute-start(bf16[768,384]{1,0:T(8,128)(2,1)S(1)} %copy-done.10), channel_id=1, source_target_pairs={{0,1},{1,2},{2,3},{3,4},{4,5},{5,6},{6,7},{7,8},{8,9},{9,10},{10,1... | collective-permute-start | bytes 1769480 | tf_op jit(solution)/shard_map/ppermute | solution.py:32
  245.4 16.9 %collective-permute-start.16 = (bf16[768,384]{1,0:T(8,128)(2,1)S(1)}, bf16[768,384]{1,0:T(8,128)(2,1)S(1)}, u32[]{:S(2)}, u32[]{:S(2)}) collective-permute-start(bf16[768,384]{1,0:T(8,128)(2,1)S(1)} %copy-done.10), channel_id=1, source_target_pairs={{0,15},{1,0},{2,1},{3,2},{4,3},{5,4},{6,5},{7,6},{8,7},{9,8},{10,9... | collective-permute-start | bytes 1769480 | tf_op jit(solution)/shard_map/ppermute | solution.py:37
  262.2 17.1 %collective-permute-start.17 = (bf16[768,384]{1,0:T(8,128)(2,1)S(1)}, bf16[768,384]{1,0:T(8,128)(2,1)S(1)}, u32[]{:S(2)}, u32[]{:S(2)}) collective-permute-start(bf16[768,384]{1,0:T(8,128)(2,1)S(1)} %collective-permute-done.15), channel_id=1, source_target_pairs={{0,1},{1,2},{2,3},{3,4},{4,5},{5,6},{6,7},{7,8},{8,9},{9,10},{10,1... | collective-permute-start | bytes 1769480 | tf_op jit(solution)/shard_map/ppermute | solution.py:32
  262.2 48.9 %copy-start.6 = (bf16[768,384]{1,0:T(8,128)(2,1)}, bf16[768,384]{1,0:T(8,128)(2,1)S(1)}, u32[]{:S(2)}) copy-start(bf16[768,384]{1,0:T(8,128)(2,1)S(1)} %collective-permute-done.16) | copy-start | bytes 1769476
  262.2 17.1 %collective-permute-start.18 = (bf16[768,384]{1,0:T(8,128)(2,1)S(1)}, bf16[768,384]{1,0:T(8,128)(2,1)S(1)}, u32[]{:S(2)}, u32[]{:S(2)}) collective-permute-start(bf16[768,384]{1,0:T(8,128)(2,1)S(1)} %collective-permute-done.16), channel_id=1, source_target_pairs={{0,15},{1,0},{2,1},{3,2},{4,3},{5,4},{6,5},{7,6},{8,7},{9,8},{10,9... | collective-permute-start | bytes 1769480 | tf_op jit(solution)/shard_map/ppermute | solution.py:37
  279.4 5.0 %copy-start.9 = (bf16[768,384]{1,0:T(8,128)(2,1)}, bf16[768,384]{1,0:T(8,128)(2,1)S(1)}, u32[]{:S(2)}) copy-start(bf16[768,384]{1,0:T(8,128)(2,1)S(1)} %collective-permute-done.17) | copy-start | bytes 1769476
  279.4 16.3 %collective-permute-start.19 = (bf16[768,384]{1,0:T(8,128)(2,1)S(1)}, bf16[768,384]{1,0:T(8,128)(2,1)S(1)}, u32[]{:S(2)}, u32[]{:S(2)}) collective-permute-start(bf16[768,384]{1,0:T(8,128)(2,1)S(1)} %collective-permute-done.17), channel_id=1, source_target_pairs={{0,1},{1,2},{2,3},{3,4},{4,5},{5,6},{6,7},{7,8},{8,9},{9,10},{10,1... | collective-permute-start | bytes 1769480 | tf_op jit(solution)/shard_map/ppermute | solution.py:32
  279.4 31.7 %copy-start.7 = (bf16[768,384]{1,0:T(8,128)(2,1)}, bf16[768,384]{1,0:T(8,128)(2,1)S(1)}, u32[]{:S(2)}) copy-start(bf16[768,384]{1,0:T(8,128)(2,1)S(1)} %collective-permute-done.18) | copy-start | bytes 1769476
  279.4 16.3 %collective-permute-start.20 = (bf16[768,384]{1,0:T(8,128)(2,1)S(1)}, bf16[768,384]{1,0:T(8,128)(2,1)S(1)}, u32[]{:S(2)}, u32[]{:S(2)}) collective-permute-start(bf16[768,384]{1,0:T(8,128)(2,1)S(1)} %collective-permute-done.18), channel_id=1, source_target_pairs={{0,15},{1,0},{2,1},{3,2},{4,3},{5,4},{6,5},{7,6},{8,7},{9,8},{10,9... | collective-permute-start | bytes 1769480 | tf_op jit(solution)/shard_map/ppermute | solution.py:37
  295.6 15.4 %collective-permute-start.21 = (bf16[768,384]{1,0:T(8,128)(2,1)S(1)}, bf16[768,384]{1,0:T(8,128)(2,1)S(1)}, u32[]{:S(2)}, u32[]{:S(2)}) collective-permute-start(bf16[768,384]{1,0:T(8,128)(2,1)S(1)} %collective-permute-done.19), channel_id=1, source_target_pairs={{0,1},{1,2},{2,3},{3,4},{4,5},{5,6},{6,7},{7,8},{8,9},{9,10},{10,1... | collective-permute-start | bytes 1769480 | tf_op jit(solution)/shard_map/ppermute | solution.py:32
  295.7 15.4 %collective-permute-start.22 = (bf16[768,384]{1,0:T(8,128)(2,1)S(1)}, bf16[768,384]{1,0:T(8,128)(2,1)}, u32[]{:S(2)}, u32[]{:S(2)}) collective-permute-start(bf16[768,384]{1,0:T(8,128)(2,1)S(1)} %collective-permute-done.20), channel_id=1, source_target_pairs={{0,15},{1,0},{2,1},{3,2},{4,3},{5,4},{6,5},{7,6},{8,7},{9,8},{10,9... | collective-permute-start | bytes 1769480 | tf_op jit(solution)/shard_map/ppermute | solution.py:37
  311.1 4.9 %copy-start.8 = (bf16[768,384]{1,0:T(8,128)(2,1)}, bf16[768,384]{1,0:T(8,128)(2,1)S(1)}, u32[]{:S(2)}) copy-start(bf16[768,384]{1,0:T(8,128)(2,1)S(1)} %collective-permute-done.21) | copy-start | bytes 1769476
  311.1 14.7 %collective-permute-start.23 = (bf16[768,384]{1,0:T(8,128)(2,1)S(1)}, bf16[768,384]{1,0:T(8,128)(2,1)}, u32[]{:S(2)}, u32[]{:S(2)}) collective-permute-start(bf16[768,384]{1,0:T(8,128)(2,1)S(1)} %collective-permute-done.21), channel_id=1, source_target_pairs={{0,1},{1,2},{2,3},{3,4},{4,5},{5,6},{6,7},{7,8},{8,9},{9,10},{10,1... | collective-permute-start | bytes 1769480 | tf_op jit(solution)/shard_map/ppermute | solution.py:32
  311.1 19.7 %collective-permute-start.24 = (bf16[768,384]{1,0:T(8,128)(2,1)}, bf16[768,384]{1,0:T(8,128)(2,1)S(1)}, u32[]{:S(2)}, u32[]{:S(2)}) collective-permute-start(bf16[768,384]{1,0:T(8,128)(2,1)} %collective-permute-done.22), channel_id=1, source_target_pairs={{0,15},{1,0},{2,1},{3,2},{4,3},{5,4},{6,5},{7,6},{8,7},{9,8},{10,9... | collective-permute-start | bytes 1769480 | tf_op jit(solution)/shard_map/ppermute | solution.py:37
  325.8 14.0 %collective-permute-start.25 = (bf16[768,384]{1,0:T(8,128)(2,1)}, bf16[768,384]{1,0:T(8,128)(2,1)}, u32[]{:S(2)}, u32[]{:S(2)}) collective-permute-start(bf16[768,384]{1,0:T(8,128)(2,1)} %collective-permute-done.23), channel_id=1, source_target_pairs={{0,1},{1,2},{2,3},{3,4},{4,5},{5,6},{6,7},{7,8},{8,9},{9,10},{10,1... | collective-permute-start | bytes 1769480 | tf_op jit(solution)/shard_map/ppermute | solution.py:32
  330.9 14.9 %collective-permute-start.26 = (bf16[768,384]{1,0:T(8,128)(2,1)S(1)}, bf16[768,384]{1,0:T(8,128)(2,1)S(1)}, u32[]{:S(2)}, u32[]{:S(2)}) collective-permute-start(bf16[768,384]{1,0:T(8,128)(2,1)S(1)} %collective-permute-done.24), channel_id=1, source_target_pairs={{0,15},{1,0},{2,1},{3,2},{4,3},{5,4},{6,5},{7,6},{8,7},{9,8},{10,9... | collective-permute-start | bytes 1769480 | tf_op jit(solution)/shard_map/ppermute | solution.py:37
  339.8 13.1 %collective-permute-start.27 = (bf16[768,384]{1,0:T(8,128)(2,1)}, bf16[768,384]{1,0:T(8,128)(2,1)S(1)}, u32[]{:S(2)}, u32[]{:S(2)}) collective-permute-start(bf16[768,384]{1,0:T(8,128)(2,1)} %collective-permute-done.25), channel_id=1, source_target_pairs={{0,1},{1,2},{2,3},{3,4},{4,5},{5,6},{6,7},{7,8},{8,9},{9,10},{10,1... | collective-permute-start | bytes 1769480 | tf_op jit(solution)/shard_map/ppermute | solution.py:32
  345.7 11.9 %collective-permute-start.28 = (bf16[768,384]{1,0:T(8,128)(2,1)S(1)}, bf16[768,384]{1,0:T(8,128)(2,1)S(1)}, u32[]{:S(2)}, u32[]{:S(2)}) collective-permute-start(bf16[768,384]{1,0:T(8,128)(2,1)S(1)} %collective-permute-done.26), channel_id=1, source_target_pairs={{0,15},{1,0},{2,1},{3,2},{4,3},{5,4},{6,5},{7,6},{8,7},{9,8},{10,9... | collective-permute-start | bytes 1769480 | tf_op jit(solution)/shard_map/ppermute | solution.py:37
  352.9 12.1 %collective-permute-start.29 = (bf16[768,384]{1,0:T(8,128)(2,1)S(1)}, bf16[768,384]{1,0:T(8,128)(2,1)S(1)}, u32[]{:S(2)}, u32[]{:S(2)}) collective-permute-start(bf16[768,384]{1,0:T(8,128)(2,1)S(1)} %collective-permute-done.27), channel_id=1, source_target_pairs={{0,1},{1,2},{2,3},{3,4},{4,5},{5,6},{6,7},{7,8},{8,9},{9,10},{10,1... | collective-permute-start | bytes 1769480 | tf_op jit(solution)/shard_map/ppermute | solution.py:32
Sparse Core Ops, SparseCore 0:
  15.6 37.7 all-gather.4
  149.0 37.4 all-gather.6
  200.1 34.1 all-gather.8
  244.2 34.2 all-gather.10
